TPU v7x, 768 devices: a whole 4x8x12 slice. The times are simulated.
768 devices in a mesh: sub: 128 (over x, z_lo, y), coarse: 6 (over z_hi, core).
Axes of the slice: x: 4, y: 8, z: 12 (z_hi: 3, z_lo: 4; z = z_hi * 4 + z_lo), core: 2. Of those that a mesh axis runs over, the one named last changes fastest.
Arguments:
- right_side: float32 [128, 64, 768], P('sub', None, 'coarse'), may hold values from -6 to 6
- local_blocks: bfloat16 [128, 2, 64, 64, 768], P('sub', None, None, None, 'coarse'), may hold values from -0.5 to 0.5
- diag_blocks: bfloat16 [128, 64, 64, 768], P('sub', None, None, 'coarse'), as said below
- iface_blocks: bfloat16 [128, 64, 64, 576], P('sub', None, None, 'coarse'), may hold values from -0.75 to 0.75
- block_cols: int32 [128, 2, 768], P('sub', None, 'coarse'), may hold values from 0 to 767
- basis: bfloat16 [128, 32, 64, 768], P('sub', None, None, 'coarse'), may hold values from -0.053955078 to 0.053955078
- coarse_inverse: float32 [4096, 4096], P('sub'), as said below
Outputs:
- solution_field: float32 [128, 64, 768], P('sub', None, 'coarse')
- residual: float32 [128, 64, 768], P('sub', None, 'coarse')
Inputs may be any that keep to these rules, and one draw needn't show every extreme that they name: `diag_blocks`: each diagonal block is 4 times the identity plus entries of magnitude at most 0.5. `coarse_inverse`: the matrix is the identity plus entries of magnitude at most 4 / sqrt(4096).
All inputs are finite; a program needn't handle non-finite values.
Results may differ from a plain program's by a relative error of at most 0.0003.
Values sent between devices are 32-bit elements; how exact they have to be, the bound alone decides.
A program may use at most 64 MiB of HBM per device.

v0:
```python
import jax
import jax.numpy as jnp
from jax import lax
from jax.sharding import PartitionSpec as P

SWEEPS = 3
ITERS = 2


HIGH = lax.Precision.HIGHEST


def from_partner(block, axis, apart):
    count = lax.axis_size(axis)
    route = []
    for low in range(count):
        high = low | 1 << apart
        if high != low and high < count:
            route += [(low, high), (high, low)]
    return lax.ppermute(block, axis, route)


def local_product(lblocks, dblock, cols, vec):
    own = jnp.einsum("ijr,jr->ir", dblock, vec, precision=HIGH, preferred_element_type=jnp.float32)
    whole = lax.all_gather(vec[None], "coarse", axis=2, tiled=True)[0]
    picked = jnp.take(whole, cols, axis=1)
    off = jnp.einsum(
        "kijr,jkr->ir", lblocks, picked, precision=HIGH, preferred_element_type=jnp.float32
    )
    return own + off


def relax(dblock, vec):
    return 0.25 * (
        2.0 * vec
        - 0.25
        * jnp.einsum("ijr,jr->ir", dblock, vec, precision=HIGH, preferred_element_type=jnp.float32)
    )


def interface_terms(fblock, vec):
    inner = fblock.shape[2] // 3
    pieces = []
    for bit in range(3):
        piece = vec[:, bit * inner : (bit + 1) * inner]
        arrived = from_partner(piece, "sub", bit)
        pieces.append(
            jnp.einsum(
                "ijm,jm->im",
                fblock[:, :, bit * inner : (bit + 1) * inner],
                arrived,
                precision=HIGH,
                preferred_element_type=jnp.float32,
            )
        )
    pieces.append(jnp.zeros((vec.shape[0], vec.shape[1] - 3 * inner), jnp.float32))
    return jnp.concatenate(pieces, axis=1)


def restrict_all(zvec, resid):
    partial_sum = jnp.einsum(
        "vjr,jr->v", zvec, resid, precision=HIGH, preferred_element_type=jnp.float32
    )
    summed = lax.psum(partial_sum, "coarse")
    return lax.all_gather(summed[None], "sub", axis=0, tiled=True).reshape(-1)


def local(right_side, local_blocks, diag_blocks, iface_blocks, block_cols, basis, coarse_inverse):
    lblocks = local_blocks[0]
    dblock = diag_blocks[0]
    fblock = iface_blocks[0]
    cols = block_cols[0]
    zvec = basis[0]
    residual = right_side[0]
    solution_field = jnp.zeros_like(residual)
    projected = restrict_all(zvec, residual)
    for step in range(ITERS):
        if step > 0:
            projected = restrict_all(zvec, residual)
        state = relax(dblock, residual)
        for sweep in range(SWEEPS - 1):
            state = state + relax(dblock, residual - local_product(lblocks, dblock, cols, state))
        weights = jnp.dot(coarse_inverse, projected, precision=HIGH)
        direction = state + jnp.einsum(
            "v,vjr->jr", weights, zvec, precision=HIGH, preferred_element_type=jnp.float32
        )
        image = local_product(lblocks, dblock, cols, direction) + interface_terms(fblock, direction)
        cross = jnp.sum(residual * image)
        square = jnp.sum(image * image)
        cross, square = lax.psum((cross, square), ("sub", "coarse"))
        alpha = cross / (square + 1e-06)
        solution_field = solution_field + alpha * direction
        residual = residual - alpha * image
    return (solution_field[None], residual[None])


def solution(mesh):
    placed = (
        P("sub", None, "coarse"),
        P("sub", None, None, None, "coarse"),
        P("sub", None, None, "coarse"),
        P("sub", None, None, "coarse"),
        P("sub", None, "coarse"),
        P("sub", None, None, "coarse"),
        P("sub", None),
    )
    return jax.shard_map(
        local,
        mesh=mesh,
        in_specs=placed,
        out_specs=(P("sub", None, "coarse"), P("sub", None, "coarse")),
        check_vma=False,
    )
```

profile of v0, /device:TPU:1, one launch (start us, length us, event | category | flops | bytes accessed | tf_op | source)
XLA Modules:
  0.0 1189.0 jit_solution(7269645044868830521)
XLA Ops:
  0.7 0.8 compare_and_fusion
  1.5 0.7 fusion.29
  2.1 0.8 copy.15
  3.1 1.8 convolution_bitcast_fusion.3
  4.8 24.1 %psum.42 = f32[1,32]{1,0:T(1,128)S(1)} all-reduce(f32[1,32]{1,0:T(1,128)S(1)} %convolution_bitcast_fusion.3), channel_id=1, replica_groups=mesh['sub'=128,'coarse'=6] {'coarse'}, use_global_device_ids=true, to_apply=%region_0.2 | all-reduce | flops 32 | bytes 256 | tf_op jit(solution)/shard_map/psum | solution.py:64
  28.9 307.1 %all-gather.6 = f32[128,1,32]{2,1,0:T(1,128)S(1)} all-gather(f32[1,1,32]{2,1,0:T(1,128)S(1)} %bitcast.354), channel_id=1, replica_groups=mesh['sub'=128,'coarse'=6] {'sub'}, dimensions={0}, use_global_device_ids=true | all-gather | bytes 16512 | tf_op jit(solution)/shard_map/all_gather | solution.py:65
  336.6 0.8 reduce.6
  338.0 1.6 fusion.3
  339.7 4.5 copy.19
  344.3 3.5 fusion.33
  347.7 74.2 %all-gather = f32[64,768]{0,1:T(8,128)S(1)} all-gather(f32[64,128]{0,1:T(8,128)S(1)} %fusion.27), channel_id=2, replica_groups=mesh['sub'=128,'coarse'=6] {'coarse'}, dimensions={1}, use_global_device_ids=true | all-gather | bytes 229376 | tf_op jit(solution)/shard_map/all_gather | solution.py:25
  422.0 1.7 fusion.34
  423.7 7.9 copy.24
  431.6 0.7 gather_fusion
  432.5 5.4 fusion.16
  437.9 1.7 fusion.35
  439.7 14.2 %all-gather.1 = f32[64,768]{0,1:T(8,128)S(1)} all-gather(f32[64,128]{0,1:T(8,128)S(1)} %fusion.26), channel_id=3, replica_groups=mesh['sub'=128,'coarse'=6] {'coarse'}, dimensions={1}, use_global_device_ids=true | all-gather | bytes 229376 | tf_op jit(solution)/shard_map/all_gather | solution.py:25
  453.8 1.7 fusion.36
  455.6 0.7 gather_fusion.1
  456.4 5.3 fusion.14
  461.7 1.7 fusion.37
  463.5 1.9 collective-permute-start
  465.4 1.9 collective-permute-start.2
  467.3 1.9 collective-permute-start.1
  469.3 14.1 %all-gather.2 = f32[64,768]{0,1:T(8,128)S(1)} all-gather(f32[64,128]{0,1:T(8,128)S(1)} %bitcast_add_fusion.1), channel_id=4, replica_groups=mesh['sub'=128,'coarse'=6] {'coarse'}, dimensions={1}, use_global_device_ids=true | all-gather | bytes 229376 | tf_op jit(solution)/shard_map/all_gather | solution.py:25
  483.4 1.7 fusion.30
  485.1 0.7 gather_fusion.2
  485.9 5.4 fusion.12
  491.3 1.7 fusion.38
  493.1 3.6 copy.42
  496.7 2.4 copy.48
  499.1 2.4 copy.45
  501.6 1.7 fusion.39
  503.3 1.6 fusion.41
  504.8 1.6 fusion.40
  506.4 0.8 multiply_reduce_fusion.2
  507.2 110.2 %all-reduce.1 = (f32[]{:T(128)}, f32[]{:T(128)}) all-reduce(f32[]{:T(128)} %get-tuple-element.12, f32[]{:T(128)} %get-tuple-element.11), channel_id=1, replica_groups=mesh['sub'=128,'coarse'=6] {'sub','coarse'}, use_global_device_ids=true, to_apply=%region_2.4 | all-reduce | flops 2 | bytes 16 | tf_op jit(solution)/shard_map/psum | solution.py:90
  618.7 0.7 convolution_bitcast_fusion.1
  619.4 13.6 %psum.45 = f32[1,32]{1,0:T(1,128)S(1)} all-reduce(f32[1,32]{1,0:T(1,128)S(1)} %convolution_bitcast_fusion.1), channel_id=1, replica_groups=mesh['sub'=128,'coarse'=6] {'coarse'}, use_global_device_ids=true, to_apply=%region_5.7 | all-reduce | flops 32 | bytes 256 | tf_op jit(solution)/shard_map/psum | solution.py:64
  633.0 302.4 %all-gather.7 = f32[128,1,32]{2,1,0:T(1,128)S(1)} all-gather(f32[1,1,32]{2,1,0:T(1,128)S(1)} %bitcast.355), channel_id=1, replica_groups=mesh['sub'=128,'coarse'=6] {'sub'}, dimensions={0}, use_global_device_ids=true | all-gather | bytes 16512 | tf_op jit(solution)/shard_map/all_gather | solution.py:65
  935.4 0.8 reduce.7
  937.5 1.7 fusion.42
  939.3 73.5 %all-gather.3 = f32[64,768]{0,1:T(8,128)S(1)} all-gather(f32[64,128]{0,1:T(8,128)S(1)} %fusion.22), channel_id=5, replica_groups=mesh['sub'=128,'coarse'=6] {'coarse'}, dimensions={1}, use_global_device_ids=true | all-gather | bytes 229376 | tf_op jit(solution)/shard_map/all_gather | solution.py:25
  1012.8 2.4 fusion.43
  1015.1 0.7 gather_fusion.3
  1016.0 5.3 fusion.10
  1021.3 1.7 fusion.44
  1023.1 14.2 %all-gather.4 = f32[64,768]{0,1:T(8,128)S(1)} all-gather(f32[64,128]{0,1:T(8,128)S(1)} %fusion.21), channel_id=6, replica_groups=mesh['sub'=128,'coarse'=6] {'coarse'}, dimensions={1}, use_global_device_ids=true | all-gather | bytes 229376 | tf_op jit(solution)/shard_map/all_gather | solution.py:25
  1037.3 1.7 fusion.45
  1039.0 0.7 gather_fusion.4
  1039.9 5.3 fusion.8
  1045.2 1.7 fusion.46
  1046.9 13.9 %all-gather.5 = f32[64,768]{0,1:T(8,128)S(1)} all-gather(f32[64,128]{0,1:T(8,128)S(1)} %bitcast_add_fusion), channel_id=7, replica_groups=mesh['sub'=128,'coarse'=6] {'coarse'}, dimensions={1}, use_global_device_ids=true | all-gather | bytes 229376 | tf_op jit(solution)/shard_map/all_gather | solution.py:25
  1060.8 1.9 collective-permute-start.3
  1062.8 0.7 gather_fusion.5
  1063.6 5.3 fusion.6
  1068.9 1.7 fusion.47
  1070.6 1.9 collective-permute-start.5
  1072.5 1.9 collective-permute-start.4
  1075.0 4.0 collective-permute-done.5
  1080.1 0.7 multiply_reduce_fusion
  1080.8 105.4 %all-reduce = (f32[]{:T(128)}, f32[]{:T(128)}) all-reduce(f32[]{:T(128)} %get-tuple-element.10, f32[]{:T(128)} %get-tuple-element.9), channel_id=1, replica_groups=mesh['sub'=128,'coarse'=6] {'sub','coarse'}, use_global_device_ids=true, to_apply=%region_7.9 | all-reduce | flops 2 | bytes 16 | tf_op jit(solution)/shard_map/psum | solution.py:90
  1187.5 0.7 copy.17
  1188.2 0.7 copy.16
  (67 shorter events, 5.1 us)
Async XLA Ops:
  0.6 336.9 %copy-start = (f32[32,4096]{1,0:T(8,128)S(1)}, f32[32,4096]{1,0:T(8,128)}, u32[]{:S(2)}) copy-start(f32[32,4096]{1,0:T(8,128)} %param.15) | copy-start | bytes 1572868
  0.6 339.1 %copy-start.8 = (bf16[1,64,64,128]{3,2,1,0:T(8,128)(2,1)S(1)}, bf16[1,64,64,128]{3,2,1,0:T(8,128)(2,1)}, u32[]{:S(2)}) copy-start(bf16[1,64,64,128]{3,2,1,0:T(8,128)(2,1)} %param.11) | copy-start | bytes 3145732
  344.2 77.7 %copy-start.4 = (bf16[64,64,128]{0,1,2:T(8,128)(2,1)S(1)}, bf16[64,64,128]{0,1,2:T(8,128)(2,1)}, u32[]{:S(2)}) copy-start(bf16[64,64,128]{0,1,2:T(8,128)(2,1)} %copy.19) | copy-start | bytes 3145732
  344.3 79.5 %copy-start.2 = (bf16[1,2,64,64,128]{4,3,2,1,0:T(8,128)(2,1)S(1)}, bf16[1,2,64,64,128]{4,3,2,1,0:T(8,128)(2,1)}, u32[]{:S(2)}) copy-start(bf16[1,2,64,64,128]{4,3,2,1,0:T(8,128)(2,1)} %param.10) | copy-start | bytes 6291460
  432.4 5.4 copy-start.5
  461.7 21.7 %copy-start.1 = (bf16[1,64,64,96]{3,2,1,0:T(8,128)(2,1)S(1)}, bf16[1,64,64,96]{3,2,1,0:T(8,128)(2,1)}, u32[]{:S(2)}) copy-start(bf16[1,64,64,96]{3,2,1,0:T(8,128)(2,1)} %param.12) | copy-start | bytes 2359300
  463.5 38.1 %collective-permute-start = (f32[64,32]{0,1:T(8,128)S(1)}, f32[64,32]{0,1:T(8,128)S(1)}, u32[]{:S(2)}, u32[]{:S(2)}) collective-permute-start(f32[64,32]{0,1:T(8,128)S(1)} %get-tuple-element.25), channel_id=1, source_target_pairs={{0,6},{6,0},{12,18},{18,12},{24,30},{30,24},{36,42},{42,36},{48,54... | collective-permute-start | bytes 24584 | tf_op jit(solution)/shard_map/ppermute | solution.py:20
  465.4 37.9 %collective-permute-start.2 = (f32[64,32]{0,1:T(8,128)S(1)}, f32[64,32]{0,1:T(8,128)S(1)}, u32[]{:S(2)}, u32[]{:S(2)}) collective-permute-start(f32[64,32]{0,1:T(8,128)S(1)} %get-tuple-element.26), channel_id=1, source_target_pairs={{0,24},{24,0},{6,30},{30,6},{12,36},{36,12},{18,42},{42,18},{48,72... | collective-permute-start | bytes 24584 | tf_op jit(solution)/shard_map/ppermute | solution.py:20
  467.3 37.5 %collective-permute-start.1 = (f32[64,32]{0,1:T(8,128)S(1)}, f32[64,32]{0,1:T(8,128)S(1)}, u32[]{:S(2)}, u32[]{:S(2)}) collective-permute-start(f32[64,32]{0,1:T(8,128)S(1)} %get-tuple-element.27), channel_id=1, source_target_pairs={{0,12},{12,0},{6,18},{18,6},{24,36},{36,24},{30,42},{42,30},{48,60... | collective-permute-start | bytes 24584 | tf_op jit(solution)/shard_map/ppermute | solution.py:20
  485.9 5.4 copy-start.6
  499.1 119.6 %copy-start.3 = (bf16[1,32,64,128]{3,2,1,0:T(8,128)(2,1)S(1)}, bf16[1,32,64,128]{3,2,1,0:T(8,128)(2,1)}, u32[]{:S(2)}) copy-start(bf16[1,32,64,128]{3,2,1,0:T(8,128)(2,1)} %param.14) | copy-start | bytes 1572868
  501.6 435.9 %copy-start.7 = (bf16[64,64,128]{0,1,2:T(8,128)(2,1)S(1)}, bf16[64,64,128]{0,1,2:T(8,128)(2,1)}, u32[]{:S(2)}) copy-start(bf16[64,64,128]{0,1,2:T(8,128)(2,1)} %copy.19) | copy-start | bytes 3145732
  1016.0 5.3 copy-start.12
  1060.8 13.6 %collective-permute-start.3 = (f32[64,32]{0,1:T(8,128)S(1)}, f32[64,32]{0,1:T(8,128)S(1)}, u32[]{:S(2)}, u32[]{:S(2)}) collective-permute-start(f32[64,32]{0,1:T(8,128)S(1)} %get-tuple-element.22), channel_id=1, source_target_pairs={{0,6},{6,0},{12,18},{18,12},{24,30},{30,24},{36,42},{42,36},{48,54... | collective-permute-start | bytes 24584 | tf_op jit(solution)/shard_map/ppermute | solution.py:20
  1068.9 5.6 copy-start.11
  1068.9 10.1 copy-start.10
  1068.9 10.7 copy-start.9
  1070.6 8.4 collective-permute-start.5
  1072.5 7.0 collective-permute-start.4
where the time goes:
time: 1190 us
  blocking collectives  1070 us (90%)
  matrix products  67.1 us (6%)
  local copies, waits for them, and re-layouts  30.3 us (3%)
    all_gather x2, blocking collectives, restrict_all(): return lax.all_gather(summed[None], 'sub', axis=0, tiled=True).reshape(-1)  610 us
    psum x2, blocking collectives, local(): cross, square = lax.psum((cross, square), ('sub', 'coarse'))  216 us
    all_gather x6, blocking collectives, local_product(): whole = lax.all_gather(vec[None], 'coarse', axis=2, tiled=True)[0]  204 us
    psum x2, blocking collectives, restrict_all(): summed = lax.psum(partial_sum, 'coarse')  37.7 us
    dot_general x6, matrix products, local_product(): jnp.einsum('kijr,jkr->ir', lblocks, picked, precision=HIGH, preferred_ele...  31.9 us
  transfers between devices with their start and end apart: 6, of which 1 were waited for; matrix products, arithmetic and copies ran while one was open for 3% of the time, Pallas kernels for 0%

commit v1 on v0

v1 whole, which is shorter than its diff:
```python
import jax
import jax.numpy as jnp
from jax import lax
from jax.experimental import pallas as pl
from jax.experimental.pallas import tpu as pltpu
from jax.sharding import PartitionSpec as P

ITERS = 2
B = 64
R = 128
NV = 32
NY, NXZ, NC = 8, 16, 6
HOLD = 2
CH = B // HOLD
F32 = jnp.float32


def kernel(
    rhs, loc, dia, ifc, cols, bas, inv,
    x_out, r_out,
    d_in, o_in, i_in, zb, ci, t0, colv,
    dt, ot, it, tmp, tmpi,
    gb, pk, wv, pv, sv, yv,
    fsend, frecv,
    rowy, rowx, rowc, dey, dex, dec,
    ldsem, gsend, grecv, fs_sem, fr_sem,
    rys, ryr, rxs, rxr, rcs, rcr,
    eys, eyr, exs, exr, ecs, ecr,
):
    sub = lax.axis_index("sub")
    me = lax.axis_index("coarse")
    xz, y = sub // NY, sub % NY
    core = me % 2
    mate = me + 1 - 2 * core
    far = [(me + 2) % NC, (me + 4) % NC]
    y_peers = [(y + d) % NY for d in range(1, NY)]
    x_peers = [(xz + d) % NXZ for d in range(1, NXZ)]
    c_peers = [(me + d) % NC for d in range(1, NC)]
    partners = [y + 1 - 2 * (y % 2), y + 2 - 4 * ((y // 2) % 2), (y + 4) % NY]
    pending = []

    loads = [
        pltpu.make_async_copy(src, dst, ldsem.at[n])
        for n, (src, dst) in enumerate(
            [
                (rhs.at[0], t0),
                (dia.at[0], d_in),
                (bas.at[0], zb),
                (cols.at[0], colv),
                (loc.at[0], o_in),
                (ifc.at[0], i_in),
                (inv, ci),
            ]
        )
    ]
    for copy in loads:
        copy.start()

    barrier = pltpu.get_barrier_semaphore()
    for q in c_peers:
        pl.semaphore_signal(barrier, inc=1, device_id=(sub, q), device_id_type=pl.DeviceIdType.MESH)
    for q in y_peers:
        pl.semaphore_signal(barrier, inc=1, device_id=(xz * NY + q, me), device_id_type=pl.DeviceIdType.MESH)
    for q in x_peers:
        pl.semaphore_signal(barrier, inc=1, device_id=(q * NY + y, me), device_id_type=pl.DeviceIdType.MESH)

    def remote(src, dst, ssem, rsem, to_sub, to_coarse):
        return pltpu.make_async_remote_copy(
            src_ref=src, dst_ref=dst, send_sem=ssem, recv_sem=rsem,
            device_id=(to_sub, to_coarse), device_id_type=pl.DeviceIdType.MESH,
        )

    def send(*args):
        copy = remote(*args)
        copy.start()
        pending.append(copy)

    def widen(src, dst):
        def step(i8, carry):
            base = pl.multiple_of(i8 * 8, 8)
            tmp[...] = src[pl.ds(base, 8)].astype(F32).reshape(8 * B, R)
            for j in range(B):
                dst[j, pl.ds(base, 8), :] = tmp[pl.ds(j, 8, stride=B), :]
            return carry
        lax.fori_loop(0, B // 8, step, 0)

    def widen_narrow(src, dst):
        width = src.shape[2]
        tmpi[...] = jnp.zeros_like(tmpi)
        def step(i8, carry):
            base = pl.multiple_of(i8 * 8, 8)
            tmpi[:, 0:width] = src[pl.ds(base, 8)].astype(F32).reshape(8 * B, width)
            for j in range(B):
                dst[j, pl.ds(base, 8), :] = tmpi[pl.ds(j, 8, stride=B), :]
            return carry
        lax.fori_loop(0, B // 8, step, 0)

    def product(acc, pairs, lo=0, hi=B):
        def step(j8, carry):
            for jj in range(8):
                j = j8 * 8 + jj
                for blocks, vec in pairs:
                    carry = carry + blocks[j] * vec[pl.ds(j, 1), :]
            return carry
        return lax.fori_loop(lo // 8, hi // 8, step, acc)

    def relax(vec_ref):
        return 0.5 * vec_ref[...] - 0.0625 * product(jnp.zeros((B, R), F32), [(dt, vec_ref)])

    lane = lax.broadcasted_iota(jnp.int32, (NV, R), 1)
    row = lax.broadcasted_iota(jnp.int32, (NV, R), 0)

    def restrict_row(vec_ref):
        vec = vec_ref[...]
        def step(v4, carry):
            for vv in range(4):
                v = v4 * 4 + vv
                part = (zb[v].astype(F32) * vec).reshape(8, 8, R)
                sv[pl.ds(pl.multiple_of(v * 8, 8), 8), :] = jnp.sum(part, axis=0)
            return carry
        lax.fori_loop(0, NV // 4, step, 0)
        total = sv[pl.ds(0, NV, stride=8), :]
        for s in range(1, 8):
            total = total + sv[pl.ds(s, NV, stride=8), :]
        column = jnp.sum(total, axis=1, keepdims=True)
        return jnp.sum(jnp.where(lane == row + (y % 4) * NV, column, 0.0), axis=0, keepdims=True)

    def extend(acc):
        def step(v4, carry):
            for vv in range(4):
                v = v4 * 4 + vv
                carry = carry + zb[v].astype(F32) * yv[pl.ds(v, 1), :]
            return carry
        return lax.fori_loop(0, NV // 4, step, acc)

    def all_y(buf, ssem, rsem):
        for q in y_peers:
            send(buf.at[y], buf.at[y], ssem.at[q], rsem.at[y], xz * NY + q, me)

    def all_x(buf, ssem, rsem):
        for q in x_peers:
            send(buf.at[xz], buf.at[xz], ssem.at[q], rsem.at[xz], q * NY + y, me)

    def all_c(buf, ssem, rsem):
        for q in c_peers:
            send(buf.at[me], buf.at[me], ssem.at[q], rsem.at[me], sub, q)

    def arrived(buf, ssem, rsem, slots):
        for q in slots:
            remote(buf.at[q], buf.at[q], ssem.at[q], rsem.at[q], sub, mate).wait_recv()

    def restrict_start(n, vec_ref):
        rowy[n, y] = restrict_row(vec_ref)
        all_y(rowy.at[n], rys.at[n], ryr.at[n])

    def restrict_turn(n):
        arrived(rowy.at[n], rys.at[n], ryr.at[n], y_peers)
        for half in range(2):
            total = rowy[n, 4 * half]
            for q in range(1, 4):
                total = total + rowy[n, 4 * half + q]
            rowx[n, xz, pl.ds(half, 1), :] = total
        all_x(rowx.at[n], rxs.at[n], rxr.at[n])

    def restrict_apply(n):
        arrived(rowx.at[n], rxs.at[n], rxr.at[n], x_peers)
        total = jnp.zeros((NV, R), F32)
        for q in range(NXZ):
            for half in range(2):
                t = 2 * q + half
                total = total + ci[:, t * R:(t + 1) * R] * rowx[n, q, pl.ds(half, 1), :]
        column = jnp.sum(total, axis=1, keepdims=True)
        rowc[n, me] = jnp.sum(jnp.where(lane == row, column, 0.0), axis=0, keepdims=True)
        all_c(rowc.at[n], rcs.at[n], rcr.at[n])

    def restrict_end(n):
        arrived(rowc.at[n], rcs.at[n], rcr.at[n], c_peers)
        total = rowc[n, 0]
        for q in range(1, NC):
            total = total + rowc[n, q]
        column = jnp.sum(jnp.where(lane == row, total, 0.0), axis=1, keepdims=True)
        yv[...] = jnp.broadcast_to(column, (NV, R))

    def dot_rows(a, b):
        first = jnp.sum(a * b, axis=0, keepdims=True)
        second = jnp.sum(b * b, axis=0, keepdims=True)
        return first, second

    def dots_start(n, a, b):
        first, second = dot_rows(a, b)
        dey[n, y, 0:1, :] = first
        dey[n, y, 1:2, :] = second
        all_y(dey.at[n], eys.at[n], eyr.at[n])

    def dots_turn(n):
        arrived(dey.at[n], eys.at[n], eyr.at[n], y_peers)
        total = dey[n, 0]
        for q in range(1, NY):
            total = total + dey[n, q]
        dex[n, xz] = total
        all_x(dex.at[n], exs.at[n], exr.at[n])

    def dots_turn_again(n):
        arrived(dex.at[n], exs.at[n], exr.at[n], x_peers)
        total = dex[n, 0]
        for q in range(1, NXZ):
            total = total + dex[n, q]
        dec[n, me] = total
        all_c(dec.at[n], ecs.at[n], ecr.at[n])

    def dots_end(n):
        arrived(dec.at[n], ecs.at[n], ecr.at[n], c_peers)
        total = dec[n, 0]
        for q in range(1, NC):
            total = total + dec[n, q]
        both = jnp.sum(total, axis=1, keepdims=True)
        return both[0:1] / (both[1:2] + 1e-06)

    def piece(g, q, h):
        return gb.at[g, q, pl.ds(h * CH, CH), :]

    def gather_start(g):
        for h in range(HOLD):
            for n, q in enumerate(far):
                send(piece(g, me, h), piece(g, me, h), gsend.at[g, n, h], grecv.at[g, me, h], sub, q)
        for h in range(HOLD):
            send(piece(g, me, h), piece(g, me, h), gsend.at[g, 2, h], grecv.at[g, me, h], sub, mate)

    def gather_wait(g, q, h):
        remote(piece(g, q, h), piece(g, q, h), gsend.at[g, 0, h], grecv.at[g, q, h], sub, mate).wait_recv()

    def gather_relay(g, h):
        for n, q in enumerate(far):
            gather_wait(g, q, h)
            send(piece(g, q, h), piece(g, q, h), gsend.at[g, 3 + n, h], grecv.at[g, q, h], sub, mate)

    def gather_use(g, h, acc):
        gather_wait(g, mate, h)
        for q in far:
            gather_wait(g, q + 1 - 2 * core, h)
        for k in range(2):
            where_from = jnp.broadcast_to(colv[k:k + 1, :], (CH, R))
            index, owner = where_from & (R - 1), where_from >> 7
            picked = jnp.zeros((CH, R), F32)
            for q in range(NC):
                values = jnp.take_along_axis(
                    gb[g, q, h * CH:(h + 1) * CH, :], index, axis=1, mode="promise_in_bounds"
                )
                picked = jnp.where(owner == q, values, picked)
            pk[k, h * CH:(h + 1) * CH, :] = picked
        return product(acc, [(ot.at[0], pk.at[0]), (ot.at[1], pk.at[1])], h * CH, (h + 1) * CH)

    def gather_product(g, acc):
        for h in range(HOLD):
            gather_relay(g, h)
            if h > 0:
                acc = gather_use(g, h - 1, acc)
        return gather_use(g, HOLD - 1, acc)

    lane16 = lax.broadcasted_iota(jnp.int32, (16, R), 1) // 32

    def interface_start(n, vec_ref):
        for q in range(3):
            packed = jnp.zeros((16, R), F32)
            for a in range(4):
                rows = vec_ref[16 * a:16 * (a + 1), :]
                if a != q:
                    rows = pltpu.roll(rows, (32 * (a - q)) % R, 1)
                packed = jnp.where(lane16 == a, rows, packed)
            fsend[n, q] = packed
            send(
                fsend.at[n, q], frecv.at[n, q], fs_sem.at[n, q], fr_sem.at[n, q],
                xz * NY + partners[q], me,
            )

    def interface_product(n, acc):
        for q in range(3):
            remote(fsend.at[n, q], frecv.at[n, q], fs_sem.at[n, q], fr_sem.at[n, q], sub, mate).wait_recv()
        for a in range(4):
            rows = jnp.zeros((16, R), F32)
            for q in range(3):
                packed = frecv[n, q]
                if a != q:
                    packed = pltpu.roll(packed, (32 * (q - a)) % R, 1)
                rows = jnp.where(lane16 == q, packed, rows)
            pv[16 * a:16 * (a + 1), :] = rows
        return product(acc, [(it, pv)])

    loads[0].wait()
    loads[1].wait()
    widen(d_in, dt)
    gb[0, me] = relax(t0)
    loads[2].wait()
    rowy[0, y] = restrict_row(t0)
    loads[3].wait()

    pl.semaphore_wait(barrier, len(c_peers) + len(y_peers) + len(x_peers))

    zero = jnp.zeros((B, R), F32)
    for n in range(ITERS):
        base = t0 if n == 0 else wv.at[0]
        g0, g1, g2 = 3 * n, 3 * n + 1, 3 * n + 2
        if n > 0:
            gb[g0, me] = relax(base)
        gather_start(g0)
        if n == 0:
            all_y(rowy.at[0], rys.at[0], ryr.at[0])
            loads[4].wait()
            widen(o_in.at[0], ot.at[0])
            widen(o_in.at[1], ot.at[1])
        else:
            restrict_start(n, base)
            dots_start(0, t0[...], base[...])
        acc = product(zero, [(dt, gb.at[g0, me])])
        restrict_turn(n)
        if n > 0:
            dots_turn(0)
        acc = gather_product(g0, acc)
        wv[2] = base[...] - acc
        gb[g1, me] = gb[g0, me] + relax(wv.at[2])
        gather_start(g1)

        acc = product(zero, [(dt, gb.at[g1, me])])
        if n == 0:
            loads[6].wait()
        restrict_apply(n)
        if n > 0:
            dots_turn_again(0)
        if n == 0:
            loads[5].wait()
            widen_narrow(i_in, it)
        acc = gather_product(g1, acc)
        wv[2] = base[...] - acc
        acc = gb[g1, me] + relax(wv.at[2])
        restrict_end(n)
        gb[g2, me] = extend(acc)
        gather_start(g2)
        interface_start(n, gb.at[g2, me])
        acc = product(zero, [(dt, gb.at[g2, me])])
        acc = interface_product(n, acc)
        acc = gather_product(g2, acc)
        if n == 0:
            wv[0] = acc
        else:
            alpha = dots_end(0)
            first = wv[0]
            res = t0[...] - alpha * first
            image = first - alpha * acc
            dots_start(1, res, image)
            step1 = gb[2, me]
            step2 = step1 - alpha * gb[5, me]
            wv[1] = res
            wv[2] = image
            dots_turn(1)
            dots_turn_again(1)
            last = dots_end(1)
            x_out[0] = alpha * step1 + last * step2
            r_out[0] = wv[1] - last * wv[2]
    for copy in pending:
        copy.wait_send()


def local(right_side, local_blocks, diag_blocks, iface_blocks, block_cols, basis, coarse_inverse):
    dma = pltpu.SemaphoreType.DMA
    vm = pltpu.VMEM
    bf = jnp.bfloat16
    shape = jax.ShapeDtypeStruct((1, B, R), F32)
    scratch = [
        vm((B, B, R), bf), vm((2, B, B, R), bf), vm((B, B, 96), bf), vm((NV, B, R), bf),
        vm((NV, NV * NXZ * NY), F32), vm((B, R), F32), vm((2, R), jnp.int32),
        vm((B, B, R), F32), vm((2, B, B, R), F32), vm((B, B, R), F32),
        vm((8 * B, R), F32), vm((8 * B, R), F32),
        vm((3 * ITERS, NC, B, R), F32), vm((2, B, R), F32), vm((3, B, R), F32), vm((B, R), F32),
        vm((NV * 8, R), F32), vm((NV, R), F32),
        vm((ITERS, 3, 16, R), F32), vm((ITERS, 3, 16, R), F32),
        vm((ITERS, NY, 1, R), F32), vm((ITERS, NXZ, 2, R), F32), vm((ITERS, NC, 1, R), F32),
        vm((ITERS, NY, 2, R), F32), vm((ITERS, NXZ, 2, R), F32), vm((ITERS, NC, 2, R), F32),
        dma((7,)), dma((3 * ITERS, 5, HOLD)), dma((3 * ITERS, NC, HOLD)),
        dma((ITERS, 3)), dma((ITERS, 3)),
    ] + [dma((ITERS, n)) for n in (NY, NY, NXZ, NXZ, NC, NC)] * 2
    return pl.pallas_call(
        kernel,
        out_shape=(shape, shape),
        in_specs=[pl.BlockSpec(memory_space=pl.ANY)] * 7,
        out_specs=(pl.BlockSpec(memory_space=pltpu.VMEM),) * 2,
        scratch_shapes=scratch,
        compiler_params=pltpu.CompilerParams(
            collective_id=0, has_side_effects=True, vmem_limit_bytes=48 * 1024 * 1024
        ),
    )(right_side, local_blocks, diag_blocks, iface_blocks, block_cols, basis, coarse_inverse)


def solution(mesh):
    placed = (
        P("sub", None, "coarse"),
        P("sub", None, None, None, "coarse"),
        P("sub", None, None, "coarse"),
        P("sub", None, None, "coarse"),
        P("sub", None, "coarse"),
        P("sub", None, None, "coarse"),
        P("sub", None),
    )
    return jax.shard_map(
        local,
        mesh=mesh,
        in_specs=placed,
        out_specs=(P("sub", None, "coarse"), P("sub", None, "coarse")),
        check_vma=False,
    )
```

time: 1190 us -> 93.1 us (0.08)
  blocking collectives: 1070 us -> 0 us
  Pallas kernels: 0 us -> 83.3 us
  matrix products: 67.1 us -> 0 us
  local copies, waits for them, and re-layouts: 30.3 us -> 8.78 us
    all_gather x8 -> x0, blocking collectives: 814 us -> none  [the longest x2 610 us: restrict_all(): return lax.all_gather(summed[None], 'sub', axis=0, tiled=True).reshape(-1)]
    psum x4 -> x0, blocking collectives: 253 us -> none  [the longest x2 216 us: local(): cross, square = lax.psum((cross, square), ('sub', 'coarse'))]
    pallas_call x0 -> x1, Pallas kernels: none -> 83.3 us  [local(): pl.pallas_call(kernel, out_shape=(shape, shape), in_specs=[pl.BlockSpec(m...]
    dot_general x30 -> x0, matrix products: 67.1 us -> none  [the longest x6 31.9 us: local_product(): jnp.einsum('kijr,jkr->ir', lblocks, picked, precision=HIGH, preferred_ele...]
    squeeze x3 -> x0, local copies, waits for them, and re-layouts: 12.5 us -> none  [the longest x1 7.89 us: local(): lblocks = local_blocks[0]]
  transfers between devices with their start and end apart: 6 -> 0, of which waited for: 1 -> 0; matrix products, arithmetic and copies ran while one was open for 3% -> 0% of each run, Pallas kernels for 0% -> 0%
where the time goes in v1:
time: 93.1 us; the launch traced here: 92.7 us
  Pallas kernels  83.3 us (89%)
  local copies, waits for them, and re-layouts  8.78 us (9%)
    pallas_call x1, Pallas kernels, local(): pl.pallas_call(kernel, out_shape=(shape, shape), in_specs=[pl.BlockSpec(m...  83.3 us
    unnamed x16, local copies, waits for them, and re-layouts  8.78 us

profile of v1, /device:TPU:1, one launch (start us, length us, event | category | flops | bytes accessed | tf_op | source)
XLA Modules:
  0.0 92.7 jit_solution(2679568154402010045)
XLA Ops:
  0.6 0.0 copy-start
  0.6 1.6 %copy-done = bf16[1,2,64,64,128]{4,3,2,1,0:T(8,128)(2,1)S(1)} copy-done((bf16[1,2,64,64,128]{4,3,2,1,0:T(8,128)(2,1)S(1)}, bf16[1,2,64,64,128]{4,3,2,1,0:T(8,128)(2,1)}, u32[]{:S(2)}) %copy-start) | copy-done | bytes 2097176
  2.2 0.0 copy-start.1
  2.2 1.2 %copy-done.1 = bf16[1,64,64,128]{3,2,1,0:T(8,128)(2,1)S(1)} copy-done((bf16[1,64,64,128]{3,2,1,0:T(8,128)(2,1)S(1)}, bf16[1,64,64,128]{3,2,1,0:T(8,128)(2,1)}, u32[]{:S(2)}) %copy-start.1) | copy-done | bytes 1048600
  3.4 0.0 copy-start.2
  3.5 1.2 %copy-done.2 = bf16[1,64,64,96]{3,2,1,0:T(8,128)(2,1)S(1)} copy-done((bf16[1,64,64,96]{3,2,1,0:T(8,128)(2,1)S(1)}, bf16[1,64,64,96]{3,2,1,0:T(8,128)(2,1)}, u32[]{:S(2)}) %copy-start.2) | copy-done | bytes 786456
  4.7 0.0 copy-start.3
  4.7 1.0 %copy-done.3 = bf16[1,32,64,128]{3,2,1,0:T(8,128)(2,1)S(1)} copy-done((bf16[1,32,64,128]{3,2,1,0:T(8,128)(2,1)S(1)}, bf16[1,32,64,128]{3,2,1,0:T(8,128)(2,1)}, u32[]{:S(2)}) %copy-start.3) | copy-done | bytes 524312
  5.7 0.0 copy-start.4
  5.7 1.0 %copy-done.4 = f32[32,4096]{1,0:T(8,128)S(1)} copy-done((f32[32,4096]{1,0:T(8,128)S(1)}, f32[32,4096]{1,0:T(8,128)}, u32[]{:S(2)}) %copy-start.4) | copy-done | bytes 524312
  6.8 0.0 copy-start.5
  6.8 0.8 copy-done.5
  7.5 0.0 copy-start.6
  7.5 0.7 copy-done.6
  8.2 83.3 %shard_map.86 = (f32[1,64,128]{2,1,0:T(8,128)S(1)}, f32[1,64,128]{2,1,0:T(8,128)S(1)}) custom-call(f32[1,64,128]{2,1,0:T(8,128)S(1)} %copy-done.5, bf16[1,2,64,64,128]{4,3,2,1,0:T(8,128)(2,1)S(1)} %copy-done, bf16[1,64,64,128]{3,2,1,0:T(8,128)(2,1)S(1)} %copy-done.1, bf16[1,64,64,96]{3,2,1,0:T(8,128)(2,1)S(1)} %copy-done.2, s32[1,2,128]{2,1,0:T(2,128)S(1)} %copy-done.6, ...), custom_call_target="tpu_custom_call" | custom-call | tf_op jit(solution)/shard_map/pallas_call | solution.py:381
  91.5 0.6 copy.11
  92.1 0.6 copy.12
Async XLA Ops:
  0.6 1.6 %copy-start = (bf16[1,2,64,64,128]{4,3,2,1,0:T(8,128)(2,1)S(1)}, bf16[1,2,64,64,128]{4,3,2,1,0:T(8,128)(2,1)}, u32[]{:S(2)}) copy-start(bf16[1,2,64,64,128]{4,3,2,1,0:T(8,128)(2,1)} %loc.1) | copy-start | bytes 6291460
  2.2 1.2 %copy-start.1 = (bf16[1,64,64,128]{3,2,1,0:T(8,128)(2,1)S(1)}, bf16[1,64,64,128]{3,2,1,0:T(8,128)(2,1)}, u32[]{:S(2)}) copy-start(bf16[1,64,64,128]{3,2,1,0:T(8,128)(2,1)} %dia.1) | copy-start | bytes 3145732
  3.4 1.2 %copy-start.2 = (bf16[1,64,64,96]{3,2,1,0:T(8,128)(2,1)S(1)}, bf16[1,64,64,96]{3,2,1,0:T(8,128)(2,1)}, u32[]{:S(2)}) copy-start(bf16[1,64,64,96]{3,2,1,0:T(8,128)(2,1)} %ifc.1) | copy-start | bytes 2359300
  4.7 1.0 %copy-start.3 = (bf16[1,32,64,128]{3,2,1,0:T(8,128)(2,1)S(1)}, bf16[1,32,64,128]{3,2,1,0:T(8,128)(2,1)}, u32[]{:S(2)}) copy-start(bf16[1,32,64,128]{3,2,1,0:T(8,128)(2,1)} %bas.1) | copy-start | bytes 1572868
  5.7 1.0 %copy-start.4 = (f32[32,4096]{1,0:T(8,128)S(1)}, f32[32,4096]{1,0:T(8,128)}, u32[]{:S(2)}) copy-start(f32[32,4096]{1,0:T(8,128)} %inv.1) | copy-start | bytes 1572868
  6.8 0.8 copy-start.5
  7.5 0.7 copy-start.6

commit v2 on v1

v2 whole, which is shorter than its diff:
```python
import jax
import jax.numpy as jnp
from jax import lax
from jax.experimental import pallas as pl
from jax.experimental.pallas import tpu as pltpu
from jax.sharding import PartitionSpec as P

ITERS = 2
B = 64
R = 128
NV = 32
NX, NZ, NY, NC = 4, 4, 8, 6
LINE, PLANE = NZ * NC, NX * NY
PITCH = B + 4
HOLD = 2
CH = B // HOLD
F32 = jnp.float32


def kernel(
    rhs, loc, dia, ifc, cols, bas, inv,
    parts, scale,
    d_in, o_in, i_in, zb, ci, cp, t0, colv,
    dt, ot, it, tmp, tmpi,
    gb, pk, wv, pv, sv, yv, zy, ow,
    fsend, frecv,
    rowl, rowp, dotl, dotp,
    ldsem, outsem, gsend, grecv, fs_sem, fr_sem, ex_send, ex_recv,
):
    sub = lax.axis_index("sub")
    me = lax.axis_index("coarse")
    xz, y = sub // NY, sub % NY
    x, z = xz // NZ, xz % NZ
    core = me % 2
    mate = me + 1 - 2 * core
    far = [(me + 2) % NC, (me + 4) % NC]
    line = []
    for dz in range(NZ):
        for dc in range(NC):
            if dz or dc:
                line.append(((x * NZ + (z + dz) % NZ) * NY + y, (me + dc) % NC))
    plane = []
    for dx in range(NX):
        for dy in range(NY):
            if dx or dy:
                plane.append(((((x + dx) % NX) * NZ + z) * NY + (y + dy) % NY, me))
    partners = [y + 1 - 2 * (y % 2), y + 2 - 4 * ((y // 2) % 2), (y + 4) % NY]
    in_line, in_plane = z * NC + me, x * NY + y
    pending = []

    loads = [
        pltpu.make_async_copy(src, dst, ldsem.at[n])
        for n, (src, dst) in enumerate(
            [
                (rhs.at[0], t0),
                (dia.at[0], d_in),
                (bas.at[0], zb),
                (cols.at[0], colv),
                (loc.at[0], o_in),
                (ifc.at[0], i_in),
                (inv, ci),
            ]
        )
    ]
    loads[0].start()
    loads[1].start()

    barrier = pltpu.get_barrier_semaphore()
    for to in line + plane:
        pl.semaphore_signal(barrier, inc=1, device_id=to, device_id_type=pl.DeviceIdType.MESH)

    def remote(src, dst, ssem, rsem, to):
        return pltpu.make_async_remote_copy(
            src_ref=src, dst_ref=dst, send_sem=ssem, recv_sem=rsem,
            device_id=to, device_id_type=pl.DeviceIdType.MESH,
        )

    def send(*args):
        copy = remote(*args)
        copy.start()
        pending.append(copy)

    def sends_done():
        while pending:
            pending.pop().wait_send()

    def widen(src, dst):
        def step(i8, carry):
            base = pl.multiple_of(i8 * 8, 8)
            for i in range(8):
                tmp[PITCH * i:PITCH * i + B, :] = src[base + i].astype(F32)
            for j in range(B):
                dst[j, pl.ds(base, 8), :] = tmp[pl.ds(j, 8, stride=PITCH), :]
            return carry
        lax.fori_loop(0, B // 8, step, 0)

    def widen_narrow(src, dst):
        width = src.shape[2]
        tmpi[...] = jnp.zeros_like(tmpi)
        def step(i8, carry):
            base = pl.multiple_of(i8 * 8, 8)
            for i in range(8):
                tmpi[PITCH * i:PITCH * i + B, 0:width] = src[base + i].astype(F32)
            for j in range(B):
                dst[j, pl.ds(base, 8), :] = tmpi[pl.ds(j, 8, stride=PITCH), :]
            return carry
        lax.fori_loop(0, B // 8, step, 0)

    def product(acc, pairs, lo=0, hi=B):
        def step(j8, carry):
            for jj in range(8):
                j = j8 * 8 + jj
                for blocks, vec in pairs:
                    carry = carry + blocks[j] * vec[pl.ds(j, 1), :]
            return carry
        return lax.fori_loop(lo // 8, hi // 8, step, acc)

    def relax(vec_ref):
        return 0.5 * vec_ref[...] - 0.0625 * product(jnp.zeros((B, R), F32), [(dt, vec_ref)])

    lane = lax.broadcasted_iota(jnp.int32, (NV, R), 1)
    row = lax.broadcasted_iota(jnp.int32, (NV, R), 0)

    def restrict_row(vec_ref):
        vec = vec_ref[...]
        def step(v4, carry):
            for vv in range(4):
                v = v4 * 4 + vv
                part = (zb[v].astype(F32) * vec).reshape(8, 8, R)
                sv[pl.ds(pl.multiple_of(v * 8, 8), 8), :] = jnp.sum(part, axis=0)
            return carry
        lax.fori_loop(0, NV // 4, step, 0)
        total = sv[pl.ds(0, NV, stride=8), :]
        for s in range(1, 8):
            total = total + sv[pl.ds(s, NV, stride=8), :]
        column = jnp.sum(total, axis=1, keepdims=True)
        return jnp.sum(jnp.where(lane == row + z * NV, column, 0.0), axis=0, keepdims=True)

    def extend(acc):
        def step(v4, carry):
            for vv in range(4):
                v = v4 * 4 + vv
                carry = carry + zb[v].astype(F32) * yv[pl.ds(v, 1), :]
            return carry
        return lax.fori_loop(0, NV // 4, step, acc)

    def exchange(k, buf, slot, devices):
        for to in devices:
            remote(buf.at[slot], buf.at[slot], ex_send.at[k], ex_recv.at[k], to).start()

    def exchanged(k, buf, devices):
        every = buf.at[pl.ds(0, len(devices))]
        copy = remote(every, every, ex_send.at[k], ex_recv.at[k], devices[0])
        copy.wait_recv()
        return copy

    def turn_inverse():
        group = lane // NV
        def step(xy, carry):
            xx, half = xy // 2, xy % 2
            tiles = [
                ci[:, pl.ds(pl.multiple_of(((xx * NZ + zz) * 2 + half) * R, R), R)] for zz in range(NZ)
            ]
            for low in range(4):
                out = jnp.zeros((NV, R), F32)
                for zz in range(NZ):
                    tile = tiles[zz]
                    if zz != low:
                        tile = pltpu.roll(tile, (NV * (zz - low)) % R, 1)
                    out = jnp.where(group == zz, tile, out)
                cp[xx * NY + half * 4 + low] = out
            return carry
        lax.fori_loop(0, 2 * NX, step, 0)

    def restrict_turn(n):
        sent = exchanged(4 * n, rowl.at[n], line)
        total = rowl[n, 0]
        for q in range(1, LINE):
            total = total + rowl[n, q]
        rowp[n, in_plane] = total
        exchange(4 * n + 1, rowp.at[n], in_plane, plane)
        sent.wait_send()

    def restrict_end(n):
        sent = exchanged(4 * n + 1, rowp.at[n], plane)
        total = cp[0] * rowp[n, 0]
        for q in range(1, PLANE):
            total = total + cp[q] * rowp[n, q]
        yv[...] = jnp.broadcast_to(jnp.sum(total, axis=1, keepdims=True), (NV, R))
        zy[...] = extend(jnp.zeros((B, R), F32))
        sent.wait_send()

    def dots_start(n, a, b):
        dotl[n, in_line, 0:1, :] = jnp.sum(a * b, axis=0, keepdims=True)
        dotl[n, in_line, 1:2, :] = jnp.sum(b * b, axis=0, keepdims=True)
        exchange(4 * n + 2, dotl.at[n], in_line, line)

    def dots_turn(n):
        sent = exchanged(4 * n + 2, dotl.at[n], line)
        total = dotl[n, 0]
        for q in range(1, LINE):
            total = total + dotl[n, q]
        dotp[n, in_plane] = total
        exchange(4 * n + 3, dotp.at[n], in_plane, plane)
        sent.wait_send()

    def dots_end(n):
        sent = exchanged(4 * n + 3, dotp.at[n], plane)
        total = dotp[n, 0]
        for q in range(1, PLANE):
            total = total + dotp[n, q]
        both = jnp.sum(total, axis=1, keepdims=True)
        return both[0:1] / (both[1:2] + 1e-06), sent

    def piece(g, q, h):
        return gb.at[g, q, pl.ds(h * CH, CH), :]

    def gather_start(g):
        for h in range(HOLD):
            for n, q in enumerate(far):
                send(piece(g, me, h), piece(g, me, h), gsend.at[g, n, h], grecv.at[g, me, h], (sub, q))
        for h in range(HOLD):
            send(piece(g, me, h), piece(g, me, h), gsend.at[g, 2, h], grecv.at[g, me, h], (sub, mate))

    def gather_wait(g, q, h):
        remote(piece(g, q, h), piece(g, q, h), gsend.at[g, 0, h], grecv.at[g, q, h], (sub, mate)).wait_recv()

    def gather_relay(g, h):
        for n, q in enumerate(far):
            gather_wait(g, q, h)
            send(piece(g, q, h), piece(g, q, h), gsend.at[g, 3 + n, h], grecv.at[g, q, h], (sub, mate))

    def gather_use(g, h, acc):
        gather_wait(g, mate, h)
        for q in far:
            gather_wait(g, q + 1 - 2 * core, h)
        for k in range(2):
            where_from = jnp.broadcast_to(colv[k:k + 1, :], (CH, R))
            index, owner = where_from & (R - 1), where_from >> 7
            picked = jnp.zeros((CH, R), F32)
            for q in range(NC):
                values = jnp.take_along_axis(
                    gb[g, q, h * CH:(h + 1) * CH, :], index, axis=1, mode="promise_in_bounds"
                )
                picked = jnp.where(owner == q, values, picked)
            pk[k, h * CH:(h + 1) * CH, :] = picked
        return product(acc, [(ot.at[0], pk.at[0]), (ot.at[1], pk.at[1])], h * CH, (h + 1) * CH)

    def gather_product(g, acc, between=None):
        for h in range(HOLD):
            gather_relay(g, h)
        if between is not None:
            between()
        for h in range(HOLD):
            acc = gather_use(g, h, acc)
        return acc

    lane16 = lax.broadcasted_iota(jnp.int32, (16, R), 1) // 32

    def interface_start(n, vec_ref):
        for q in range(3):
            packed = jnp.zeros((16, R), F32)
            for a in range(4):
                rows = vec_ref[16 * a:16 * (a + 1), :]
                if a != q:
                    rows = pltpu.roll(rows, (32 * (a - q)) % R, 1)
                packed = jnp.where(lane16 == a, rows, packed)
            fsend[n, q] = packed
            send(
                fsend.at[n, q], frecv.at[n, q], fs_sem.at[n, q], fr_sem.at[n, q],
                (xz * NY + partners[q], me),
            )

    def interface_product(n, acc):
        for q in range(3):
            remote(fsend.at[n, q], frecv.at[n, q], fs_sem.at[n, q], fr_sem.at[n, q], (sub, mate)).wait_recv()
        for a in range(4):
            rows = jnp.zeros((16, R), F32)
            for q in range(3):
                packed = frecv[n, q]
                if a != q:
                    packed = pltpu.roll(packed, (32 * (q - a)) % R, 1)
                rows = jnp.where(lane16 == q, packed, rows)
            pv[16 * a:16 * (a + 1), :] = rows
        return product(acc, [(it, pv)])

    loads[0].wait()
    loads[1].wait()
    for copy in loads[2:]:
        copy.start()
    widen(d_in, dt)
    gb[0, me] = relax(t0)
    pl.semaphore_wait(barrier, len(line) + len(plane))

    zero = jnp.zeros((B, R), F32)
    for n in range(ITERS):
        base = t0 if n == 0 else wv.at[0]
        g0, g1, g2 = 3 * n, 3 * n + 1, 3 * n + 2
        if n > 0:
            gb[g0, me] = relax(base)
        gather_start(g0)
        if n == 0:
            loads[2].wait()
        rowl[n, in_line] = restrict_row(base)
        exchange(4 * n, rowl.at[n], in_line, line)
        if n > 0:
            dots_start(0, t0[...], base[...])
        acc = product(zero, [(dt, gb.at[g0, me])])
        if n == 0:
            loads[3].wait()
            loads[4].wait()
            widen(o_in.at[0], ot.at[0])
            widen(o_in.at[1], ot.at[1])
        acc = gather_product(g0, acc)
        wv[2] = base[...] - acc
        gb[g1, me] = gb[g0, me] + relax(wv.at[2])
        gather_start(g1)
        restrict_turn(n)
        acc = product(zero, [(dt, gb.at[g1, me])])
        if n == 0:
            loads[6].wait()
            turn_inverse()
            loads[5].wait()
            widen_narrow(i_in, it)
        else:
            dots_turn(0)
        acc = gather_product(g1, acc, lambda: restrict_end(n))
        wv[2] = base[...] - acc
        gb[g2, me] = gb[g1, me] + relax(wv.at[2]) + zy[...]
        gather_start(g2)
        interface_start(n, gb.at[g2, me])
        acc = product(zero, [(dt, gb.at[g2, me])])
        if n > 0:
            alpha, sent = dots_end(0)
            first = wv[0]
            res = t0[...] - alpha * first
            step1 = gb[2, me]
            wv[1] = res
            ow[0] = alpha * step1
            ow[1] = step1 - alpha * gb[5, me]
            ow[2] = res
            sent.wait_send()
        acc = interface_product(n, acc)
        acc = gather_product(g2, acc)
        if n == 0:
            wv[0] = acc
        else:
            image = wv[0] - alpha * acc
            dots_start(1, wv[1], image)
            ow[3] = image
            copy = pltpu.make_async_copy(ow, parts, outsem)
            copy.start()
            sends_done()
            dots_turn(1)
            copy.wait()
            last, sent = dots_end(1)
            scale[...] = jnp.broadcast_to(last, (1, R))
            sent.wait_send()


def local(right_side, local_blocks, diag_blocks, iface_blocks, block_cols, basis, coarse_inverse):
    dma = pltpu.SemaphoreType.DMA
    vm = pltpu.VMEM
    bf = jnp.bfloat16
    turned = PITCH * 7 + B
    scratch = [
        vm((B, B, R), bf), vm((2, B, B, R), bf), vm((B, B, 96), bf), vm((NV, B, R), bf),
        vm((NV, PLANE * R), F32), vm((PLANE, NV, R), F32), vm((B, R), F32), vm((2, R), jnp.int32),
        vm((B, B, R), F32), vm((2, B, B, R), F32), vm((B, B, R), F32),
        vm((turned, R), F32), vm((turned, R), F32),
        vm((3 * ITERS, NC, B, R), F32), vm((2, B, R), F32), vm((3, B, R), F32), vm((B, R), F32),
        vm((NV * 8, R), F32), vm((NV, R), F32), vm((B, R), F32), vm((4, B, R), F32),
        vm((ITERS, 3, 16, R), F32), vm((ITERS, 3, 16, R), F32),
        vm((ITERS, LINE, 1, R), F32), vm((ITERS, PLANE, 1, R), F32),
        vm((ITERS, LINE, 2, R), F32), vm((ITERS, PLANE, 2, R), F32),
        dma((7,)), dma, dma((3 * ITERS, 5, HOLD)), dma((3 * ITERS, NC, HOLD)),
        dma((ITERS, 3)), dma((ITERS, 3)), dma((4 * ITERS,)), dma((4 * ITERS,)),
    ]
    parts, scale = pl.pallas_call(
        kernel,
        out_shape=(jax.ShapeDtypeStruct((4, B, R), F32), jax.ShapeDtypeStruct((1, R), F32)),
        in_specs=[pl.BlockSpec(memory_space=pl.ANY)] * 7,
        out_specs=(pl.BlockSpec(memory_space=pl.ANY), pl.BlockSpec(memory_space=pltpu.VMEM)),
        scratch_shapes=scratch,
        compiler_params=pltpu.CompilerParams(
            collective_id=0, has_side_effects=True, vmem_limit_bytes=67043328
        ),
    )(right_side, local_blocks, diag_blocks, iface_blocks, block_cols, basis, coarse_inverse)
    last = scale[:, None, :]
    return parts[0:1] + last * parts[1:2], parts[2:3] - last * parts[3:4]


def solution(mesh):
    placed = (
        P("sub", None, "coarse"),
        P("sub", None, None, None, "coarse"),
        P("sub", None, None, "coarse"),
        P("sub", None, None, "coarse"),
        P("sub", None, "coarse"),
        P("sub", None, None, "coarse"),
        P("sub", None),
    )
    return jax.shard_map(
        local,
        mesh=mesh,
        in_specs=placed,
        out_specs=(P("sub", None, "coarse"), P("sub", None, "coarse")),
        check_vma=False,
    )
```

time: 93.1 us -> 82.1 us (0.88)
  local copies, waits for them, and re-layouts: 8.78 us -> 0 us
  Pallas kernels: 83.3 us -> 79.7 us
  other arithmetic: 0 us -> 1.44 us
    unnamed x16 -> x0, local copies, waits for them, and re-layouts: 8.78 us -> none
    pallas_call x1, Pallas kernels: 83.3 us -> 79.7 us  [local(): pl.pallas_call(kernel, out_shape=(jax.ShapeDtypeStruct((4, B, R), F32), j...]
    sub x0 -> x1, other arithmetic: none -> 1.44 us  [local(): return (parts[0:1] + last * parts[1:2], parts[2:3] - last * parts[3:4])]
where the time goes in v2:
time: 82.1 us; the launch traced here: 81.8 us
  Pallas kernels  79.7 us (97%)
  other arithmetic  1.44 us (2%)
    pallas_call x1, Pallas kernels, local(): pl.pallas_call(kernel, out_shape=(jax.ShapeDtypeStruct((4, B, R), F32), j...  79.7 us

profile of v2, /device:TPU:1, one launch (start us, length us, event | category | flops | bytes accessed | tf_op | source)
XLA Modules:
  0.0 81.8 jit_solution(8789325102790009947)
XLA Ops:
  0.6 79.7 %shard_map.86 = (f32[4,64,128]{2,1,0:T(8,128)}, f32[1,128]{1,0:T(1,128)}) custom-call(f32[1,64,128]{2,1,0:T(8,128)} %rhs.1, bf16[1,2,64,64,128]{4,3,2,1,0:T(8,128)(2,1)} %loc.1, bf16[1,64,64,128]{3,2,1,0:T(8,128)(2,1)} %dia.1, bf16[1,64,64,96]{3,2,1,0:T(8,128)(2,1)} %ifc.1, s32[1,2,128]{2,1,0:T(2,128)} %cols.1, bf16[1,32,64,128]{3,2,1,0:T(8,128)(2,1)} %bas.1, ...), custom_call_target="tpu_custom_call" | custom-call | tf_op jit(solution)/shard_map/pallas_call | solution.py:379
  80.4 1.4 %multiply_subtract_fusion = (f32[1,64,128]{2,1,0:T(8,128)}, f32[1,64,128]{2,1,0:T(8,128)}) fusion(f32[4,64,128]{2,1,0:T(8,128)} %get-tuple-element.4, f32[128]{0:T(128)} %bitcast.1), kind=kLoop, calls=%fused_computation | loop fusion | flops 32768 | bytes 197120 | tf_op jit(solution)/shard_map/sub | solution.py:390

commit v3 on v2

--- a/solution.py
+++ b/solution.py
@@ -12,8 +12,8 @@
 NX, NZ, NY, NC = 4, 4, 8, 6
 LINE, PLANE = NZ * NC, NX * NY
 PITCH = B + 4
-HOLD = 2
-CH = B // HOLD
+CUTS = ((0, 48), (48, 16))
+HOLD = len(CUTS)
 F32 = jnp.float32
 
 
@@ -25,7 +25,7 @@
     gb, pk, wv, pv, sv, yv, zy, ow,
     fsend, frecv,
     rowl, rowp, dotl, dotp,
-    ldsem, outsem, gsend, grecv, fs_sem, fr_sem, ex_send, ex_recv,
+    ldsem, outsem, gsend, farsem, matesem, fs_sem, fr_sem, ex_send, ex_recv,
 ):
     sub = lax.axis_index("sub")
     me = lax.axis_index("coarse")
@@ -46,7 +46,6 @@
                 plane.append(((((x + dx) % NX) * NZ + z) * NY + (y + dy) % NY, me))
     partners = [y + 1 - 2 * (y % 2), y + 2 - 4 * ((y // 2) % 2), (y + 4) % NY]
     in_line, in_plane = z * NC + me, x * NY + y
-    pending = []
 
     loads = [
         pltpu.make_async_copy(src, dst, ldsem.at[n])
@@ -75,14 +74,10 @@
             device_id=to, device_id_type=pl.DeviceIdType.MESH,
         )
 
-    def send(*args):
-        copy = remote(*args)
-        copy.start()
-        pending.append(copy)
-
     def sends_done():
-        while pending:
-            pending.pop().wait_send()
+        every = gb.at[pl.ds(0, 5)]
+        remote(every, every, gsend, farsem.at[0, 0, 0], (sub, mate)).wait_send()
+        remote(fsend, frecv, fs_sem, fr_sem.at[0, 0], (sub, mate)).wait_send()
 
     def widen(src, dst):
         def step(i8, carry):
@@ -115,8 +110,15 @@
             return carry
         return lax.fori_loop(lo // 8, hi // 8, step, acc)
 
-    def relax(vec_ref):
-        return 0.5 * vec_ref[...] - 0.0625 * product(jnp.zeros((B, R), F32), [(dt, vec_ref)])
+    def relax(vec_ref, h):
+        lo, rows = CUTS[h]
+        def step(j8, carry):
+            for jj in range(8):
+                j = j8 * 8 + jj
+                carry = carry + dt[j, lo:lo + rows, :] * vec_ref[pl.ds(j, 1), :]
+            return carry
+        total = lax.fori_loop(0, B // 8, step, jnp.zeros((rows, R), F32))
+        return 0.5 * vec_ref[lo:lo + rows, :] - 0.0625 * total
 
     lane = lax.broadcasted_iota(jnp.int32, (NV, R), 1)
     row = lax.broadcasted_iota(jnp.int32, (NV, R), 0)
@@ -213,44 +215,44 @@
         return both[0:1] / (both[1:2] + 1e-06), sent
 
     def piece(g, q, h):
-        return gb.at[g, q, pl.ds(h * CH, CH), :]
-
-    def gather_start(g):
-        for h in range(HOLD):
+        return gb.at[g, q, pl.ds(CUTS[h][0], CUTS[h][1]), :]
+
+    def gather_send(g, h, to, sem, q=me):
+        remote(piece(g, q, h), piece(g, q, h), gsend, sem, to).start()
+
+    def gather_start(g, rows_of):
+        for h, (lo, rows) in enumerate(CUTS):
+            gb[g, me, lo:lo + rows, :] = rows_of(h)
             for n, q in enumerate(far):
-                send(piece(g, me, h), piece(g, me, h), gsend.at[g, n, h], grecv.at[g, me, h], (sub, q))
-        for h in range(HOLD):
-            send(piece(g, me, h), piece(g, me, h), gsend.at[g, 2, h], grecv.at[g, me, h], (sub, mate))
-
-    def gather_wait(g, q, h):
-        remote(piece(g, q, h), piece(g, q, h), gsend.at[g, 0, h], grecv.at[g, q, h], (sub, mate)).wait_recv()
+                gather_send(g, h, (sub, q), farsem.at[g, n, h])
+            gather_send(g, h, (sub, mate), matesem.at[g, h])
 
     def gather_relay(g, h):
         for n, q in enumerate(far):
-            gather_wait(g, q, h)
-            send(piece(g, q, h), piece(g, q, h), gsend.at[g, 3 + n, h], grecv.at[g, q, h], (sub, mate))
+            remote(piece(g, q, h), piece(g, q, h), gsend, farsem.at[g, 1 - n, h], (sub, mate)).wait_recv()
+            gather_send(g, h, (sub, mate), matesem.at[g, h], q)
 
     def gather_use(g, h, acc):
-        gather_wait(g, mate, h)
-        for q in far:
-            gather_wait(g, q + 1 - 2 * core, h)
+        lo, rows = CUTS[h]
+        three = gb.at[g, pl.ds(0, 3), pl.ds(lo, rows), :]
+        remote(three, three, gsend, matesem.at[g, h], (sub, mate)).wait_recv()
         for k in range(2):
-            where_from = jnp.broadcast_to(colv[k:k + 1, :], (CH, R))
+            where_from = jnp.broadcast_to(colv[k:k + 1, :], (rows, R))
             index, owner = where_from & (R - 1), where_from >> 7
-            picked = jnp.zeros((CH, R), F32)
+            picked = jnp.zeros((rows, R), F32)
             for q in range(NC):
                 values = jnp.take_along_axis(
-                    gb[g, q, h * CH:(h + 1) * CH, :], index, axis=1, mode="promise_in_bounds"
+                    gb[g, q, lo:lo + rows, :], index, axis=1, mode="promise_in_bounds"
                 )
                 picked = jnp.where(owner == q, values, picked)
-            pk[k, h * CH:(h + 1) * CH, :] = picked
-        return product(acc, [(ot.at[0], pk.at[0]), (ot.at[1], pk.at[1])], h * CH, (h + 1) * CH)
+            pk[k, lo:lo + rows, :] = picked
+        return product(acc, [(ot.at[0], pk.at[0]), (ot.at[1], pk.at[1])], lo, lo + rows)
 
     def gather_product(g, acc, between=None):
         for h in range(HOLD):
             gather_relay(g, h)
         if between is not None:
-            between()
+            acc = between(acc)
         for h in range(HOLD):
             acc = gather_use(g, h, acc)
         return acc
@@ -266,14 +268,13 @@
                     rows = pltpu.roll(rows, (32 * (a - q)) % R, 1)
                 packed = jnp.where(lane16 == a, rows, packed)
             fsend[n, q] = packed
-            send(
-                fsend.at[n, q], frecv.at[n, q], fs_sem.at[n, q], fr_sem.at[n, q],
-                (xz * NY + partners[q], me),
-            )
+            remote(
+                fsend.at[n, q], frecv.at[n, q], fs_sem, fr_sem.at[n, q], (xz * NY + partners[q], me)
+            ).start()
 
     def interface_product(n, acc):
         for q in range(3):
-            remote(fsend.at[n, q], frecv.at[n, q], fs_sem.at[n, q], fr_sem.at[n, q], (sub, mate)).wait_recv()
+            remote(fsend.at[n, q], frecv.at[n, q], fs_sem, fr_sem.at[n, q], (sub, mate)).wait_recv()
         for a in range(4):
             rows = jnp.zeros((16, R), F32)
             for q in range(3):
@@ -289,16 +290,13 @@
     for copy in loads[2:]:
         copy.start()
     widen(d_in, dt)
-    gb[0, me] = relax(t0)
     pl.semaphore_wait(barrier, len(line) + len(plane))
 
     zero = jnp.zeros((B, R), F32)
     for n in range(ITERS):
         base = t0 if n == 0 else wv.at[0]
         g0, g1, g2 = 3 * n, 3 * n + 1, 3 * n + 2
-        if n > 0:
-            gb[g0, me] = relax(base)
-        gather_start(g0)
+        gather_start(g0, lambda h: relax(base, h))
         if n == 0:
             loads[2].wait()
         rowl[n, in_line] = restrict_row(base)
@@ -313,8 +311,7 @@
             widen(o_in.at[1], ot.at[1])
         acc = gather_product(g0, acc)
         wv[2] = base[...] - acc
-        gb[g1, me] = gb[g0, me] + relax(wv.at[2])
-        gather_start(g1)
+        gather_start(g1, lambda h: gb[g0, me, CUTS[h][0]:sum(CUTS[h]), :] + relax(wv.at[2], h))
         restrict_turn(n)
         acc = product(zero, [(dt, gb.at[g1, me])])
         if n == 0:
@@ -324,10 +321,15 @@
             widen_narrow(i_in, it)
         else:
             dots_turn(0)
-        acc = gather_product(g1, acc, lambda: restrict_end(n))
+
+        def restricted(acc):
+            restrict_end(n)
+            return acc
+
+        acc = gather_product(g1, acc, restricted)
         wv[2] = base[...] - acc
-        gb[g2, me] = gb[g1, me] + relax(wv.at[2]) + zy[...]
-        gather_start(g2)
+        zy[...] = gb[g1, me] + zy[...]
+        gather_start(g2, lambda h: zy[CUTS[h][0]:sum(CUTS[h]), :] + relax(wv.at[2], h))
         interface_start(n, gb.at[g2, me])
         acc = product(zero, [(dt, gb.at[g2, me])])
         if n > 0:
@@ -340,8 +342,7 @@
             ow[1] = step1 - alpha * gb[5, me]
             ow[2] = res
             sent.wait_send()
-        acc = interface_product(n, acc)
-        acc = gather_product(g2, acc)
+        acc = gather_product(g2, acc, lambda acc: interface_product(n, acc))
         if n == 0:
             wv[0] = acc
         else:
@@ -373,8 +374,8 @@
         vm((ITERS, 3, 16, R), F32), vm((ITERS, 3, 16, R), F32),
         vm((ITERS, LINE, 1, R), F32), vm((ITERS, PLANE, 1, R), F32),
         vm((ITERS, LINE, 2, R), F32), vm((ITERS, PLANE, 2, R), F32),
-        dma((7,)), dma, dma((3 * ITERS, 5, HOLD)), dma((3 * ITERS, NC, HOLD)),
-        dma((ITERS, 3)), dma((ITERS, 3)), dma((4 * ITERS,)), dma((4 * ITERS,)),
+        dma((7,)), dma, dma, dma((3 * ITERS, 2, HOLD)), dma((3 * ITERS, HOLD)),
+        dma, dma((ITERS, 3)), dma((4 * ITERS,)), dma((4 * ITERS,)),
     ]
     parts, scale = pl.pallas_call(
         kernel,

time: 82.1 us -> 80.4 us (0.979)
  Pallas kernels: 79.7 us -> 78.1 us
    pallas_call x1, Pallas kernels: 79.7 us -> 78.1 us  [local(): pl.pallas_call(kernel, out_shape=(jax.ShapeDtypeStruct((4, B, R), F32), j...]
where the time goes in v3:
time: 80.4 us; the launch traced here: 80.2 us
  Pallas kernels  78.1 us (97%)
  other arithmetic  1.44 us (2%)
    pallas_call x1, Pallas kernels, local(): pl.pallas_call(kernel, out_shape=(jax.ShapeDtypeStruct((4, B, R), F32), j...  78.1 us

profile of v3, /device:TPU:1, one launch (start us, length us, event | category | flops | bytes accessed | tf_op | source)
XLA Modules:
  0.0 80.2 jit_solution(7005382650179931537)
XLA Ops:
  0.6 78.1 %shard_map.86 = (f32[4,64,128]{2,1,0:T(8,128)}, f32[1,128]{1,0:T(1,128)}) custom-call(f32[1,64,128]{2,1,0:T(8,128)} %rhs.1, bf16[1,2,64,64,128]{4,3,2,1,0:T(8,128)(2,1)} %loc.1, bf16[1,64,64,128]{3,2,1,0:T(8,128)(2,1)} %dia.1, bf16[1,64,64,96]{3,2,1,0:T(8,128)(2,1)} %ifc.1, s32[1,2,128]{2,1,0:T(2,128)} %cols.1, bf16[1,32,64,128]{3,2,1,0:T(8,128)(2,1)} %bas.1, ...), custom_call_target="tpu_custom_call" | custom-call | tf_op jit(solution)/shard_map/pallas_call | solution.py:380
  78.8 1.4 %multiply_subtract_fusion = (f32[1,64,128]{2,1,0:T(8,128)}, f32[1,64,128]{2,1,0:T(8,128)}) fusion(f32[4,64,128]{2,1,0:T(8,128)} %get-tuple-element.4, f32[128]{0:T(128)} %bitcast.1), kind=kLoop, calls=%fused_computation | loop fusion | flops 32768 | bytes 197120 | tf_op jit(solution)/shard_map/sub | solution.py:391

commit v4 on v3

--- a/solution.py
+++ b/solution.py
@@ -232,25 +232,31 @@
             remote(piece(g, q, h), piece(g, q, h), gsend, farsem.at[g, 1 - n, h], (sub, mate)).wait_recv()
             gather_send(g, h, (sub, mate), matesem.at[g, h], q)
 
-    def gather_use(g, h, acc):
+    def gather_pick(g, h, owners, first):
         lo, rows = CUTS[h]
-        three = gb.at[g, pl.ds(0, 3), pl.ds(lo, rows), :]
-        remote(three, three, gsend, matesem.at[g, h], (sub, mate)).wait_recv()
         for k in range(2):
             where_from = jnp.broadcast_to(colv[k:k + 1, :], (rows, R))
             index, owner = where_from & (R - 1), where_from >> 7
-            picked = jnp.zeros((rows, R), F32)
-            for q in range(NC):
+            picked = jnp.zeros((rows, R), F32) if first else pk[k, lo:lo + rows, :]
+            for q in owners:
                 values = jnp.take_along_axis(
                     gb[g, q, lo:lo + rows, :], index, axis=1, mode="promise_in_bounds"
                 )
                 picked = jnp.where(owner == q, values, picked)
             pk[k, lo:lo + rows, :] = picked
+
+    def gather_use(g, h, acc):
+        lo, rows = CUTS[h]
+        three = gb.at[g, pl.ds(0, 3), pl.ds(lo, rows), :]
+        remote(three, three, gsend, matesem.at[g, h], (sub, mate)).wait_recv()
+        gather_pick(g, h, [mate] + [q + 1 - 2 * core for q in far], False)
         return product(acc, [(ot.at[0], pk.at[0]), (ot.at[1], pk.at[1])], lo, lo + rows)
 
     def gather_product(g, acc, between=None):
         for h in range(HOLD):
             gather_relay(g, h)
+        for h in range(HOLD):
+            gather_pick(g, h, [me] + far, True)
         if between is not None:
             acc = between(acc)
         for h in range(HOLD):

time: 80.4 us -> 80.7 us (level)
  no operation moved by 1% of the time
where the time goes in v4:
time: 80.7 us; the launch traced here: 80.5 us
  Pallas kernels  78.4 us (97%)
  other arithmetic  1.44 us (2%)
    pallas_call x1, Pallas kernels, local(): pl.pallas_call(kernel, out_shape=(jax.ShapeDtypeStruct((4, B, R), F32), j...  78.4 us

profile of v4, /device:TPU:1, one launch (start us, length us, event | category | flops | bytes accessed | tf_op | source)
XLA Modules:
  0.0 80.5 jit_solution(6194371814490358031)
XLA Ops:
  0.6 78.4 %shard_map.86 = (f32[4,64,128]{2,1,0:T(8,128)}, f32[1,128]{1,0:T(1,128)}) custom-call(f32[1,64,128]{2,1,0:T(8,128)} %rhs.1, bf16[1,2,64,64,128]{4,3,2,1,0:T(8,128)(2,1)} %loc.1, bf16[1,64,64,128]{3,2,1,0:T(8,128)(2,1)} %dia.1, bf16[1,64,64,96]{3,2,1,0:T(8,128)(2,1)} %ifc.1, s32[1,2,128]{2,1,0:T(2,128)} %cols.1, bf16[1,32,64,128]{3,2,1,0:T(8,128)(2,1)} %bas.1, ...), custom_call_target="tpu_custom_call" | custom-call | tf_op jit(solution)/shard_map/pallas_call | solution.py:386
  79.0 1.4 %multiply_subtract_fusion = (f32[1,64,128]{2,1,0:T(8,128)}, f32[1,64,128]{2,1,0:T(8,128)}) fusion(f32[4,64,128]{2,1,0:T(8,128)} %get-tuple-element.4, f32[128]{0:T(128)} %bitcast.1), kind=kLoop, calls=%fused_computation | loop fusion | flops 32768 | bytes 197120 | tf_op jit(solution)/shard_map/sub | solution.py:397
